TPU v7x, 32 devices: a whole 2x2x4 slice. The times are simulated.
32 devices in a mesh: seq: 16 (over z, y, x), head: 2 (over core).
Axes of the slice: x: 2, y: 2, z: 4, core: 2. Of those that a mesh axis runs over, the one named last changes fastest.
Arguments:
- tokens: bfloat16 [16, 1024, 3072], P('seq', None, 'head'), may hold values from -6 to 6
- fast_state: float32 [16, 8, 192, 2304], P('seq', 'head'), may hold values from -6 to 6
- momentum: float32 [16, 8, 192, 2304], P('seq', 'head'), may hold values from -1.8 to 1.8
- init_fast: bfloat16 [8, 192, 2304], P('head'), may hold values from -6 to 6
- past_keys: bfloat16 [16, 2048, 1536], P('seq', None, 'head'), may hold values from -6 to 6
- past_values: bfloat16 [16, 2048, 1536], P('seq', None, 'head'), may hold values from -6 to 6
- qkv_weight: bfloat16 [3, 3072, 1536], P(None, 'seq', 'head'), may hold values from -0.109375 to 0.109375
- rate_weight: bfloat16 [3072, 8], P(None, 'head'), may hold values from -0.109375 to 0.109375
- out_weight: bfloat16 [1536, 3072], P('head'), may hold values from -0.15625 to 0.15625
- prompt_begins: int32 [2, 16], replicated, may hold values 0 or 1
Outputs:
- mixed: bfloat16 [16, 1024, 3072], P('seq', None, 'head')
- fast_out: float32 [16, 8, 192, 2304], P('seq', 'head')
- momentum_out: float32 [16, 8, 192, 2304], P('seq', 'head')
All inputs are finite; a program needn't handle non-finite values.
Results may differ from a plain program's by a relative error of at most 0.015.
Values may be sent and summed in bfloat16 or wider, within the bound.
A program may use at most 192 MiB of HBM per device.

v0:
```python
import functools
import math

import jax
import jax.numpy as jnp
from jax import lax
from jax.experimental import pallas as pl
from jax.experimental.pallas import tpu as pltpu
from jax.sharding import PartitionSpec as P

momentum_decay = 0.9
rate_scale = 0.3
epsilon = 1e-06
f32 = jnp.float32
bf16 = jnp.bfloat16


def passed_along(block, axis, distance):
    n = lax.axis_size(axis)
    return lax.ppermute(block, axis, [((i - distance) % n, i) for i in range(n)])


def unit_rows(matrix):
    matrix = matrix.astype(f32)
    return matrix * lax.rsqrt(jnp.mean(matrix * matrix, axis=-1, keepdims=True) + epsilon)


def mm(a, b, ca, cb):
    return lax.dot_general(a, b, (((ca,), (cb,)), ((), ())), preferred_element_type=f32)


def fast_kernel(steps, span, begins, q, k, v, rate, fast, mom, init, applied, fast_out, mom_out):
    group, hd, three = fast.shape
    hid = three // 3
    inv_bound = 1.0 / math.sqrt(hd)
    inv_hidden = 1.0 / math.sqrt(hid)
    for h in range(group):
        cols = slice(h * hd, (h + 1) * hd)
        w = fast[h]
        m = mom[h]
        for s in range(steps):
            rows = slice(s * span, (s + 1) * span)
            fresh = begins[s] > 0
            w = jnp.where(fresh, init[h].astype(f32), w)
            m = jnp.where(fresh, 0.0, m)
            wb = w.astype(bf16)
            up = wb[:, : 2 * hid]
            down = wb[:, 2 * hid :]
            xq = (unit_rows(q[rows, cols]) * inv_bound).astype(bf16)
            ab = mm(xq, up, 1, 0)
            a = ab[:, :hid]
            hq = (a * jax.nn.sigmoid(a) * ab[:, hid:]).astype(bf16)
            applied[rows, cols] = mm(hq, down, 1, 1) * inv_hidden
            y = (unit_rows(k[rows, cols]) * inv_bound).astype(bf16)
            ab = mm(y, up, 1, 0)
            a = ab[:, :hid]
            b = ab[:, hid:]
            sg = jax.nn.sigmoid(a)
            act = a * sg
            g = (-rate[rows, h : h + 1] * v[rows, cols].astype(f32)).astype(bf16)
            grad_down = mm(g, (act * b).astype(bf16), 0, 0) * inv_hidden
            e = mm(g, down, 1, 0) * inv_hidden
            da = (e * b * sg * (1.0 + a * (1.0 - sg))).astype(bf16)
            db = (e * act).astype(bf16)
            grad = jnp.concatenate([mm(y, da, 0, 0), mm(y, db, 0, 0), grad_down], axis=1)
            m = momentum_decay * m + grad
            w = w - m
            w = w * lax.rsqrt(jnp.mean(w * w, axis=0, keepdims=True) + epsilon)
        fast_out[h] = w.astype(bf16)
        mom_out[h] = m.astype(bf16)


def attend_kernel(steps, span, hd, begins, q, k, v, past_k, past_v, applied, mix):
    window = past_k.shape[0]
    blocks = window // span
    bound = math.sqrt(hd)
    for h in range(q.shape[1] // hd):
        cols = slice(h * hd, (h + 1) * hd)
        keys = []
        values = []
        ones = jnp.ones((span, 64), bf16)
        for c in range(blocks + steps):
            kr, vr, at = (past_k, past_v, c) if c < blocks else (k, v, c - blocks)
            rows = slice(at * span, (at + 1) * span)
            keys.append(unit_rows(kr[rows, cols]).astype(bf16))
            values.append(jnp.concatenate([vr[rows, cols], ones], axis=1))
        for s in range(steps):
            rows = slice(s * span, (s + 1) * span)
            qn = unit_rows(q[rows, cols]).astype(bf16)
            acc = jnp.zeros((span, hd + 64), f32)
            row = lax.broadcasted_iota(jnp.int32, (span, span), 0)
            col = lax.broadcasted_iota(jnp.int32, (span, span), 1)
            for c in range(s, s + blocks + 1):
                dead = jnp.int32(0)
                for t in range(max(0, c - blocks + 1), s + 1):
                    dead = jnp.maximum(dead, begins[t])
                shift = jnp.where(dead > 0, -1e30, -bound)
                p = jnp.exp(mm(qn, keys[c], 1, 1) * (1.0 / bound) + shift)
                if c == s:
                    p = jnp.where(col > row, p, 0.0)
                if c == s + blocks:
                    p = jnp.where(col <= row, p, 0.0)
                acc = acc + mm(p.astype(bf16), values[c], 1, 0)
            out = acc[:, :hd] / acc[:, hd : hd + 1]
            mix[rows, cols] = (out + applied[rows, cols]).astype(bf16)


def gathered_features(spans):
    n_head = lax.axis_size("head")
    mine = lax.axis_index("head")
    span, width = spans[0].shape
    features = jnp.zeros((span * len(spans), width * n_head), spans[0].dtype)
    for s, part in enumerate(spans):
        for d in range(n_head):
            got = part if d == 0 else passed_along(part, "head", d)
            owner = lax.rem(mine - d + n_head, n_head)
            features = lax.dynamic_update_slice(features, got, (s * span, owner * width))
    return features


def layer(
    tokens,
    fast_state,
    momentum,
    init_fast,
    past_keys,
    past_values,
    qkv_weight,
    rate_weight,
    out_weight,
    prompt_begins,
):
    n = lax.axis_size("seq")
    me = lax.axis_index("seq")
    steps = prompt_begins.shape[0]
    total = tokens.shape[1]
    span = total // steps
    window = past_keys.shape[1]
    heads, hd, three = fast_state.shape[1:]
    group = 2 if heads % 2 == 0 else heads
    wide = group * hd

    weights = lax.all_gather(qkv_weight, "seq", axis=1, tiled=True)
    spans = [tokens[0, :span]]
    for s in range(1, steps):
        spans.append(passed_along(tokens[0, s * span : (s + 1) * span], "seq", -s))
    features = gathered_features(spans)
    q, k, v = [
        jnp.dot(features, weights[c], preferred_element_type=f32).astype(bf16) for c in range(3)
    ]
    rates = (
        rate_scale
        * jax.nn.softplus(jnp.dot(features, rate_weight, preferred_element_type=f32))
    ).astype(bf16).astype(f32)
    begins = jnp.stack([prompt_begins[s, (me + s) % n] for s in range(steps)])

    smem = pl.BlockSpec(memory_space=pltpu.SMEM)

    def columns(rows, g):
        return pl.BlockSpec((rows, wide), lambda i, g=g: (0, g))

    def state(g):
        return pl.BlockSpec((None, group, hd, three), lambda i, g=g: (0, g, 0, 0))

    params = pltpu.CompilerParams(vmem_limit_bytes=58 * 1024 * 1024)
    applied = []
    sent = []
    for g in range(heads // group):
        a, w, m = pl.pallas_call(
            functools.partial(fast_kernel, steps, span),
            grid=(1,),
            in_specs=[
                smem,
                columns(total, g),
                columns(total, g),
                columns(total, g),
                pl.BlockSpec((None, total, group), lambda i, g=g: (g, 0, 0)),
                state(g),
                state(g),
                pl.BlockSpec((group, hd, three), lambda i, g=g: (g, 0, 0)),
            ],
            out_specs=[
                pl.BlockSpec((total, wide), lambda i: (0, 0)),
                pl.BlockSpec((group, hd, three), lambda i: (0, 0, 0)),
                pl.BlockSpec((group, hd, three), lambda i: (0, 0, 0)),
            ],
            out_shape=[
                jax.ShapeDtypeStruct((total, wide), f32),
                jax.ShapeDtypeStruct((group, hd, three), bf16),
                jax.ShapeDtypeStruct((group, hd, three), bf16),
            ],
            compiler_params=params,
        )(
            begins,
            q,
            k,
            v,
            rates.reshape(total, heads // group, group).transpose(1, 0, 2),
            fast_state,
            momentum,
            init_fast,
        )
        applied.append(a)
        sent.append((passed_along(w, "seq", steps - 1), passed_along(m, "seq", steps - 1)))

    mixes = []
    for g in range(heads // group):
        mixes.append(
            pl.pallas_call(
                functools.partial(attend_kernel, steps, span, hd),
                grid=(1,),
                in_specs=[
                    smem,
                    columns(total, g),
                    columns(total, g),
                    columns(total, g),
                    columns(window, g),
                    columns(window, g),
                    pl.BlockSpec((total, wide), lambda i: (0, 0)),
                ],
                out_specs=pl.BlockSpec((total, wide), lambda i: (0, 0)),
                out_shape=jax.ShapeDtypeStruct((total, wide), bf16),
                compiler_params=params,
            )(begins, q, k, v, past_keys[0], past_values[0], applied[g])
        )
    mix = jnp.concatenate(mixes, axis=1)
    placed = [mix[:span]]
    for s in range(1, steps):
        placed.append(passed_along(mix[s * span : (s + 1) * span], "seq", s))
    reduced = []
    for part in placed:
        partial_value = jnp.dot(part, out_weight, preferred_element_type=f32).astype(bf16)
        reduced.append(
            lax.psum_scatter(partial_value, "head", scatter_dimension=1, tiled=True)
        )
    mixed = jnp.concatenate(reduced, axis=0)
    fast_out = jnp.concatenate([w for w, _ in sent], axis=0).astype(f32)
    mom_out = jnp.concatenate([m for _, m in sent], axis=0).astype(f32)
    return (mixed[None], fast_out[None], mom_out[None])


def solution(mesh):
    in_specs = (
        P("seq", None, "head"),
        P("seq", "head", None, None),
        P("seq", "head", None, None),
        P("head", None, None),
        P("seq", None, "head"),
        P("seq", None, "head"),
        P(None, "seq", "head"),
        P(None, "head"),
        P("head", None),
        P(),
    )
    out_specs = (P("seq", None, "head"), P("seq", "head", None, None), P("seq", "head", None, None))
    return jax.shard_map(layer, mesh=mesh, in_specs=in_specs, out_specs=out_specs, check_vma=False)
```

profile of v0, /device:TPU:0, one launch (start us, length us, event | category | flops | bytes accessed | tf_op | source)
XLA Modules:
  0.0 499.3 jit_solution(4997525275646237227)
XLA Ops:
  7.2 0.0 copy-start
  7.2 0.0 all-gather.2.cloned.1.call-start
  7.2 0.7 all-gather.2.cloned.1.call-update
  7.9 0.0 reduce-scatter.3.cloned.1.call-start
  8.0 3.2 slice_bitcast_fusion.12
  11.2 7.0 %collective-permute-start.1 = (bf16[512,1536]{1,0:T(8,128)(2,1)S(1)}, bf16[512,1536]{1,0:T(8,128)(2,1)}, u32[]{:S(2)}, u32[]{:S(2)}) collective-permute-start(bf16[512,1536]{1,0:T(8,128)(2,1)S(1)} %get-tuple-element.15), channel_id=1, source_target_pairs={{2,0},{4,2},{6,4},{8,6},{10,8},{12,10},{14,12},{16,14},{18,16},{20... | collective-permute-start | bytes 4718600 | tf_op jit(solution)/shard_map/ppermute | solution.py:20
  18.2 52.6 %collective-permute-done.1 = bf16[512,1536]{1,0:T(8,128)(2,1)} collective-permute-done((bf16[512,1536]{1,0:T(8,128)(2,1)S(1)}, bf16[512,1536]{1,0:T(8,128)(2,1)}, u32[]{:S(2)}, u32[]{:S(2)}) %collective-permute-start.1) | collective-permute-done | bytes 1572896 | tf_op jit(solution)/shard_map/ppermute | solution.py:20
  70.8 0.6 constant_dynamic-slice_fusion
  71.4 1.9 pad_add_fusion.begins
  73.3 0.8 broadcast_in_dim.8
  74.1 0.2 constant_dynamic-update-slice_fusion.3
  74.3 1.6 constant_dynamic-update-slice_fusion.2
  75.9 1.9 constant_dynamic-update-slice_fusion.1
  77.8 1.6 constant_dynamic-update-slice_fusion
  79.4 0.0 copy-start.2
  79.4 2.7 copy-done.2
  82.1 1.7 fusion.10
  83.9 1.4 copy.13
  85.2 121.0 %all-gather.2.cloned.1.call-done = bf16[3,3072,768]{2,1,0:T(8,128)(2,1)} async-done(((bf16[3,192,768]{2,1,0:T(8,128)(2,1)}), bf16[3,3072,768]{2,1,0:T(8,128)(2,1)}) %all-gather.2.cloned.1.call-update) | async-done | bytes 14155792 | tf_op jit(solution)/shard_map/all_gather | solution.py:143
  206.3 9.5 %fusion.3.q = bf16[1024,768]{1,0:T(8,128)(2,1)} fusion(bf16[1024,3072]{1,0:T(8,128)(2,1)} %copy-done.2, bf16[3,3072,768]{2,1,0:T(8,128)(2,1)} %all-gather.2.cloned.1.call-done), kind=kOutput, calls=%fused_computation.11 | convolution fusion | flops 4832624640 | bytes 12582912 | tf_op jit(solution)/shard_map/dot_general | solution.py:149
  215.8 1.1 copy-done.8
  216.8 6.2 %fusion.4.k = bf16[1024,768]{1,0:T(8,128)(2,1)} fusion(bf16[1024,3072]{1,0:T(8,128)(2,1)S(1)} %copy-done.3, bf16[3,3072,768]{2,1,0:T(8,128)(2,1)S(1)} %copy-done.8), kind=kOutput, calls=%fused_computation.12 | convolution fusion | flops 4832624640 | bytes 12582912 | tf_op jit(solution)/shard_map/dot_general | solution.py:149
  223.0 6.3 %fusion.5.v = bf16[1024,768]{1,0:T(8,128)(2,1)} fusion(bf16[1024,3072]{1,0:T(8,128)(2,1)S(1)} %copy-done.3, bf16[3,3072,768]{2,1,0:T(8,128)(2,1)S(1)} %copy-done.8), kind=kOutput, calls=%fused_computation.13 | convolution fusion | flops 4832624640 | bytes 12582912 | tf_op jit(solution)/shard_map/dot_general | solution.py:149
  229.3 17.2 %shard_map.123 = (f32[1024,384]{1,0:T(8,128)}, bf16[2,192,2304]{2,1,0:T(8,128)(2,1)}, bf16[2,192,2304]{2,1,0:T(8,128)(2,1)}) custom-call(s32[2]{0:T(128)} %pad_add_fusion.begins, bf16[1024,768]{1,0:T(8,128)(2,1)} %fusion.3.q, bf16[1024,768]{1,0:T(8,128)(2,1)} %fusion.4.k, bf16[1024,768]{1,0:T(8,128)(2,1)} %fusion.5.v, f32[2,1024,2]{2,1,0:T(8,128)} %bitcast.46, ...), custom_call_target="tpu_custom_call" | custom-call | tf_op jit(solution)/shard_map/pallas_call | solution.py:169
  246.5 17.4 %shard_map.121 = (f32[1024,384]{1,0:T(8,128)}, bf16[2,192,2304]{2,1,0:T(8,128)(2,1)}, bf16[2,192,2304]{2,1,0:T(8,128)(2,1)}) custom-call(s32[2]{0:T(128)} %pad_add_fusion.begins, bf16[1024,768]{1,0:T(8,128)(2,1)} %fusion.3.q, bf16[1024,768]{1,0:T(8,128)(2,1)} %fusion.4.k, bf16[1024,768]{1,0:T(8,128)(2,1)} %fusion.5.v, f32[2,1024,2]{2,1,0:T(8,128)} %bitcast.47, ...), custom_call_target="tpu_custom_call" | custom-call | tf_op jit(solution)/shard_map/pallas_call | solution.py:169
  263.9 14.3 %shard_map.124 = bf16[1024,384]{1,0:T(8,128)(2,1)} custom-call(s32[2]{0:T(128)} %pad_add_fusion.begins, bf16[1024,768]{1,0:T(8,128)(2,1)} %fusion.3.q, bf16[1024,768]{1,0:T(8,128)(2,1)} %fusion.4.k, bf16[1024,768]{1,0:T(8,128)(2,1)} %fusion.5.v, bf16[2048,768]{1,0:T(8,128)(2,1)} %bitcast.42, bf16[2048,768]{1,0:T(8,128)(2,1)} %bitcast.44, ...), custom_call_target="tpu_custom_call" | custom-call | tf_op jit(solution)/shard_map/pallas_call | solution.py:209
  278.2 14.2 %shard_map.122 = bf16[1024,384]{1,0:T(8,128)(2,1)} custom-call(s32[2]{0:T(128)} %pad_add_fusion.begins, bf16[1024,768]{1,0:T(8,128)(2,1)} %fusion.3.q, bf16[1024,768]{1,0:T(8,128)(2,1)} %fusion.4.k, bf16[1024,768]{1,0:T(8,128)(2,1)} %fusion.5.v, bf16[2048,768]{1,0:T(8,128)(2,1)} %bitcast.43, bf16[2048,768]{1,0:T(8,128)(2,1)} %bitcast.45, ...), custom_call_target="tpu_custom_call" | custom-call | tf_op jit(solution)/shard_map/pallas_call | solution.py:209
  292.4 6.8 %convolution_convert_fusion.1 = bf16[512,3072]{1,0:T(8,128)(2,1)} fusion(bf16[768,3072]{1,0:T(8,128)(2,1)} %param.18, bf16[1024,384]{1,0:T(8,128)(2,1)} %shard_map.122, bf16[1024,384]{1,0:T(8,128)(2,1)S(1)} %copy-done.5), kind=kOutput, calls=%fused_computation.7 | convolution fusion | flops 2419064832 | bytes 9437184 | tf_op jit(solution)/shard_map/dot_general | solution.py:232
  299.1 0.0 reduce-scatter.3.cloned.1.call-update
  299.2 0.0 reduce-scatter.5.cloned.1.call-start
  299.2 1.1 copy-done.6
  300.3 0.1 pad_maximum_fusion
  300.3 0.0 copy-start.9
  300.4 1.5 collective-permute-start.3
  301.9 20.7 %collective-permute-done.3 = bf16[512,768]{1,0:T(8,128)(2,1)S(1)} collective-permute-done((bf16[512,768]{1,0:T(8,128)(2,1)S(1)}, bf16[512,768]{1,0:T(8,128)(2,1)S(1)}, u32[]{:S(2)}, u32[]{:S(2)}) %collective-permute-start.3) | collective-permute-done | bytes 786464 | tf_op jit(solution)/shard_map/ppermute | solution.py:20
  322.6 6.4 %convolution_convert_fusion = bf16[512,3072]{1,0:T(8,128)(2,1)} fusion(bf16[512,768]{1,0:T(8,128)(2,1)S(1)} %collective-permute-done.3, bf16[768,3072]{1,0:T(8,128)(2,1)} %param.18), kind=kOutput, calls=%fused_computation.6 | convolution fusion | flops 2417491968 | bytes 8650752 | tf_op jit(solution)/shard_map/dot_general | solution.py:232
  329.0 0.0 reduce-scatter.5.cloned.1.call-update
  329.0 0.1 collective-permute-start.5
  329.1 0.2 collective-permute-start.4
  329.3 0.1 collective-permute-start.7
  329.4 1.9 collective-permute-start.6
  331.3 43.1 %collective-permute-done.5 = bf16[2,192,2304]{2,1,0:T(8,128)(2,1)S(1)} collective-permute-done((bf16[2,192,2304]{2,1,0:T(8,128)(2,1)}, bf16[2,192,2304]{2,1,0:T(8,128)(2,1)S(1)}, u32[]{:S(2)}, u32[]{:S(2)}) %collective-permute-start.5) | collective-permute-done | bytes 1769504 | tf_op jit(solution)/shard_map/ppermute | solution.py:20
  374.3 37.9 %collective-permute-done.4 = bf16[2,192,2304]{2,1,0:T(8,128)(2,1)S(1)} collective-permute-done((bf16[2,192,2304]{2,1,0:T(8,128)(2,1)}, bf16[2,192,2304]{2,1,0:T(8,128)(2,1)S(1)}, u32[]{:S(2)}, u32[]{:S(2)}) %collective-permute-start.4) | collective-permute-done | bytes 1769504 | tf_op jit(solution)/shard_map/ppermute | solution.py:20
  412.3 3.4 maximum_convert_fusion
  415.7 34.5 %collective-permute-done.7 = bf16[2,192,2304]{2,1,0:T(8,128)(2,1)S(1)} collective-permute-done((bf16[2,192,2304]{2,1,0:T(8,128)(2,1)S(1)}, bf16[2,192,2304]{2,1,0:T(8,128)(2,1)S(1)}, u32[]{:S(2)}, u32[]{:S(2)}) %collective-permute-start.7) | collective-permute-done | bytes 1769504 | tf_op jit(solution)/shard_map/ppermute | solution.py:20
  450.2 35.2 %collective-permute-done.6 = bf16[2,192,2304]{2,1,0:T(8,128)(2,1)S(1)} collective-permute-done((bf16[2,192,2304]{2,1,0:T(8,128)(2,1)}, bf16[2,192,2304]{2,1,0:T(8,128)(2,1)S(1)}, u32[]{:S(2)}, u32[]{:S(2)}) %collective-permute-start.6) | collective-permute-done | bytes 1769504 | tf_op jit(solution)/shard_map/ppermute | solution.py:20
  485.4 3.4 maximum_convert_fusion.1
  488.8 3.7 maximum_bitcast_fusion
  (21 shorter events, 0.1 us)
Async XLA Ops:
  7.2 74.9 %copy-start = (bf16[3072,4]{0,1:T(4,128)(2,1)S(1)}, bf16[3072,4]{0,1:T(4,128)(2,1)}, u32[]{:S(2)}) copy-start(bf16[3072,4]{0,1:T(4,128)(2,1)} %param.17) | copy-start | bytes 73732
  7.2 63.6 %copy-start.7 = (s32[2,16]{1,0:T(2,128)S(1)}, s32[2,16]{1,0:T(2,128)}, u32[]{:S(2)}) copy-start(s32[2,16]{1,0:T(2,128)} %param.19) | copy-start | bytes 388
  7.2 199.1 %all-gather.2.cloned.1.call-start = ((), (), s32[]{:S(2)}) async-start(), calls=%async_computation.2 | async-start | bytes 15040512 | tf_op jit(solution)/shard_map/all_gather | solution.py:143
  7.9 480.9 %reduce-scatter.3.cloned.1.call-start = ((), (), s32[]{:S(2)}) async-start(), calls=%async_computation.3 | async-start | bytes 4718592 | tf_op jit(solution)/shard_map/reduce_scatter | solution.py:234
  11.2 62.8 %copy-start.4 = (bf16[1,1024,1536]{2,1,0:T(8,128)(2,1)S(1)}, bf16[1,1024,1536]{2,1,0:T(8,128)(2,1)}, u32[]{:S(2)}) copy-start(bf16[1,1024,1536]{2,1,0:T(8,128)(2,1)} %param.10) | copy-start | bytes 9437188
  11.2 59.6 %collective-permute-start.1 = (bf16[512,1536]{1,0:T(8,128)(2,1)S(1)}, bf16[512,1536]{1,0:T(8,128)(2,1)}, u32[]{:S(2)}, u32[]{:S(2)}) collective-permute-start(bf16[512,1536]{1,0:T(8,128)(2,1)S(1)} %get-tuple-element.15), channel_id=1, source_target_pairs={{2,0},{4,2},{6,4},{8,6},{10,8},{12,10},{14,12},{16,14},{18,16},{20... | collective-permute-start | bytes 4718600 | tf_op jit(solution)/shard_map/ppermute | solution.py:20
  18.2 56.1 %collective-permute-start = (bf16[512,1536]{1,0:T(8,128)(2,1)}, bf16[512,1536]{1,0:T(8,128)(2,1)}, u32[]{:S(2)}, u32[]{:S(2)}) collective-permute-start(bf16[512,1536]{1,0:T(8,128)(2,1)} %get-tuple-element.16), channel_id=1, source_target_pairs={{1,0},{0,1},{3,2},{2,3},{5,4},{4,5},{7,6},{6,7},{9,8},{8,9},{11,10... | collective-permute-start | bytes 4718600 | tf_op jit(solution)/shard_map/ppermute | solution.py:20
  70.8 7.0 %collective-permute-start.2 = (bf16[512,1536]{1,0:T(8,128)(2,1)}, bf16[512,1536]{1,0:T(8,128)(2,1)}, u32[]{:S(2)}, u32[]{:S(2)}) collective-permute-start(bf16[512,1536]{1,0:T(8,128)(2,1)} %collective-permute-done.1), channel_id=1, source_target_pairs={{1,0},{0,1},{3,2},{2,3},{5,4},{4,5},{7,6},{6,7},{9,8},{8,9},{11,10... | collective-permute-start | bytes 4718600 | tf_op jit(solution)/shard_map/ppermute | solution.py:20
  79.4 2.7 copy-start.2
  206.2 9.5 %copy-start.3 = (bf16[1024,3072]{1,0:T(8,128)(2,1)S(1)}, bf16[1024,3072]{1,0:T(8,128)(2,1)}, u32[]{:S(2)}) copy-start(bf16[1024,3072]{1,0:T(8,128)(2,1)} %copy-done.2) | copy-start | bytes 18874372
  206.2 10.6 %copy-start.8 = (bf16[3,3072,768]{2,1,0:T(8,128)(2,1)S(1)}, bf16[3,3072,768]{2,1,0:T(8,128)(2,1)}, u32[]{:S(2)}) copy-start(bf16[3,3072,768]{2,1,0:T(8,128)(2,1)} %all-gather.2.cloned.1.call-done) | copy-start | bytes 42467332
  278.2 14.2 %copy-start.5 = (bf16[1024,384]{1,0:T(8,128)(2,1)S(1)}, bf16[1024,384]{1,0:T(8,128)(2,1)}, u32[]{:S(2)}) copy-start(bf16[1024,384]{1,0:T(8,128)(2,1)} %shard_map.124) | copy-start | bytes 2359300
  299.1 1.1 copy-start.6
  299.2 189.7 %reduce-scatter.5.cloned.1.call-start = ((), (), s32[]{:S(2)}) async-start(), calls=%async_computation.4 | async-start | bytes 4718592 | tf_op jit(solution)/shard_map/reduce_scatter | solution.py:234
  300.3 29.0 %copy-start.9 = (bf16[2,192,2304]{2,1,0:T(8,128)(2,1)S(1)}, bf16[2,192,2304]{2,1,0:T(8,128)(2,1)}, u32[]{:S(2)}) copy-start(bf16[2,192,2304]{2,1,0:T(8,128)(2,1)} %get-tuple-element.14) | copy-start | bytes 5308420
  300.4 22.2 %collective-permute-start.3 = (bf16[512,768]{1,0:T(8,128)(2,1)S(1)}, bf16[512,768]{1,0:T(8,128)(2,1)S(1)}, u32[]{:S(2)}, u32[]{:S(2)}) collective-permute-start(bf16[512,768]{1,0:T(8,128)(2,1)S(1)} %pad_maximum_fusion), channel_id=1, source_target_pairs={{30,0},{0,2},{2,4},{4,6},{6,8},{8,10},{10,12},{12,14},{14,16},{16,... | collective-permute-start | bytes 2359304 | tf_op jit(solution)/shard_map/ppermute | solution.py:20
  329.0 45.3 %collective-permute-start.5 = (bf16[2,192,2304]{2,1,0:T(8,128)(2,1)}, bf16[2,192,2304]{2,1,0:T(8,128)(2,1)S(1)}, u32[]{:S(2)}, u32[]{:S(2)}) collective-permute-start(bf16[2,192,2304]{2,1,0:T(8,128)(2,1)} %get-tuple-element.12), channel_id=1, source_target_pairs={{30,0},{0,2},{2,4},{4,6},{6,8},{8,10},{10,12},{12,14},{14,16},{16,... | collective-permute-start | bytes 5308424 | tf_op jit(solution)/shard_map/ppermute | solution.py:20
  329.1 83.2 %collective-permute-start.4 = (bf16[2,192,2304]{2,1,0:T(8,128)(2,1)}, bf16[2,192,2304]{2,1,0:T(8,128)(2,1)S(1)}, u32[]{:S(2)}, u32[]{:S(2)}) collective-permute-start(bf16[2,192,2304]{2,1,0:T(8,128)(2,1)} %get-tuple-element.11), channel_id=1, source_target_pairs={{30,0},{0,2},{2,4},{4,6},{6,8},{8,10},{10,12},{12,14},{14,16},{16,... | collective-permute-start | bytes 5308424 | tf_op jit(solution)/shard_map/ppermute | solution.py:20
  329.3 120.9 %collective-permute-start.7 = (bf16[2,192,2304]{2,1,0:T(8,128)(2,1)S(1)}, bf16[2,192,2304]{2,1,0:T(8,128)(2,1)S(1)}, u32[]{:S(2)}, u32[]{:S(2)}) collective-permute-start(bf16[2,192,2304]{2,1,0:T(8,128)(2,1)S(1)} %copy-done.9), channel_id=1, source_target_pairs={{30,0},{0,2},{2,4},{4,6},{6,8},{8,10},{10,12},{12,14},{14,16},{16,... | collective-permute-start | bytes 5308424 | tf_op jit(solution)/shard_map/ppermute | solution.py:20
  329.4 156.0 %collective-permute-start.6 = (bf16[2,192,2304]{2,1,0:T(8,128)(2,1)}, bf16[2,192,2304]{2,1,0:T(8,128)(2,1)S(1)}, u32[]{:S(2)}, u32[]{:S(2)}) collective-permute-start(bf16[2,192,2304]{2,1,0:T(8,128)(2,1)} %get-tuple-element.13), channel_id=1, source_target_pairs={{30,0},{0,2},{2,4},{4,6},{6,8},{8,10},{10,12},{12,14},{14,16},{16,... | collective-permute-start | bytes 5308424 | tf_op jit(solution)/shard_map/ppermute | solution.py:20
  485.4 7.2 %copy-start.1 = (bf16[3072,4]{0,1:T(4,128)(2,1)S(1)}, bf16[3072,4]{0,1:T(4,128)(2,1)}, u32[]{:S(2)}) copy-start(bf16[3072,4]{0,1:T(4,128)(2,1)} %param.17) | copy-start | bytes 73732
Sparse Core Ops, SparseCore 0:
  10.7 195.5 all-gather.1
  299.3 9.1 reduce-scatter.2
  329.1 7.1 reduce-scatter.4
where the time goes:
time: 506 us; the launch traced here: 499 us
  waiting for transfers between devices  346 us (68%)
  Pallas kernels  63.1 us (12%)
  matrix products  36.9 us (7%)
  local copies, waits for them, and re-layouts  16.1 us (3%)
  between operations  14.1 us (3%)
  other arithmetic  12.5 us (2%)
  starting transfers between devices  10.9 us (2%)
    ppermute x8, waiting for transfers between devices, passed_along(): lax.ppermute(block, axis, [((i - distance) % n, i) for i in range(n)])  224 us
    all_gather x1, waiting for transfers between devices, layer(): weights = lax.all_gather(qkv_weight, 'seq', axis=1, tiled=True)  121 us
    pallas_call x2, Pallas kernels, layer(): pl.pallas_call(functools.partial(fast_kernel, steps, span), grid=(1,), in...  34.6 us
    pallas_call x2, Pallas kernels, layer(): pl.pallas_call(functools.partial(attend_kernel, steps, span, hd), grid=(1...  28.5 us
    dot_general x3, matrix products, layer(): jnp.dot(features, weights[c], preferred_element_type=f32).astype(bf16)  21.9 us
    dot_general x2, matrix products, layer(): jnp.dot(part, out_weight, preferred_element_type=f32).astype(bf16)  13.2 us
    ppermute x8, starting transfers between devices, passed_along(): lax.ppermute(block, axis, [((i - distance) % n, i) for i in range(n)])  10.7 us
  transfers between devices with their start and end apart: 11, of which 7 were waited for; matrix products, arithmetic and copies ran while one was open for 6% of the time, Pallas kernels for 0%

commit v1 on v0

--- a/solution.py
+++ b/solution.py
@@ -29,7 +29,7 @@
     return lax.dot_general(a, b, (((ca,), (cb,)), ((), ())), preferred_element_type=f32)
 
 
-def fast_kernel(steps, span, begins, q, k, v, rate, fast, mom, init, applied, fast_out, mom_out):
+def fast_kernel(steps, span, begins, k, v, rate, fast, mom, init, used, fast_out, mom_out):
     group, hd, three = fast.shape
     hid = three // 3
     inv_bound = 1.0 / math.sqrt(hd)
@@ -46,11 +46,7 @@
             wb = w.astype(bf16)
             up = wb[:, : 2 * hid]
             down = wb[:, 2 * hid :]
-            xq = (unit_rows(q[rows, cols]) * inv_bound).astype(bf16)
-            ab = mm(xq, up, 1, 0)
-            a = ab[:, :hid]
-            hq = (a * jax.nn.sigmoid(a) * ab[:, hid:]).astype(bf16)
-            applied[rows, cols] = mm(hq, down, 1, 1) * inv_hidden
+            used[s, h] = wb
             y = (unit_rows(k[rows, cols]) * inv_bound).astype(bf16)
             ab = mm(y, up, 1, 0)
             a = ab[:, :hid]
@@ -70,10 +66,12 @@
         mom_out[h] = m.astype(bf16)
 
 
-def attend_kernel(steps, span, hd, begins, q, k, v, past_k, past_v, applied, mix):
+def attend_kernel(steps, span, hd, begins, q, k, v, past_k, past_v, used, mix):
     window = past_k.shape[0]
     blocks = window // span
     bound = math.sqrt(hd)
+    hid = used.shape[3] // 3
+    inv_hidden = 1.0 / math.sqrt(hid)
     for h in range(q.shape[1] // hd):
         cols = slice(h * hd, (h + 1) * hd)
         keys = []
@@ -86,7 +84,13 @@
             values.append(jnp.concatenate([vr[rows, cols], ones], axis=1))
         for s in range(steps):
             rows = slice(s * span, (s + 1) * span)
-            qn = unit_rows(q[rows, cols]).astype(bf16)
+            qf = unit_rows(q[rows, cols])
+            qn = qf.astype(bf16)
+            xq = (qf * (1.0 / bound)).astype(bf16)
+            ab = mm(xq, used[s, h, :, : 2 * hid], 1, 0)
+            a = ab[:, :hid]
+            hq = (a * jax.nn.sigmoid(a) * ab[:, hid:]).astype(bf16)
+            applied = mm(hq, used[s, h, :, 2 * hid :], 1, 1) * inv_hidden
             acc = jnp.zeros((span, hd + 64), f32)
             row = lax.broadcasted_iota(jnp.int32, (span, span), 0)
             col = lax.broadcasted_iota(jnp.int32, (span, span), 1)
@@ -102,7 +106,118 @@
                     p = jnp.where(col <= row, p, 0.0)
                 acc = acc + mm(p.astype(bf16), values[c], 1, 0)
             out = acc[:, :hd] / acc[:, hd : hd + 1]
-            mix[rows, cols] = (out + applied[rows, cols]).astype(bf16)
+            mix[rows, cols] = (out + applied).astype(bf16)
+
+
+def grid_of(n):
+    across = 2 if n % 2 == 0 else 1
+    up = 2 if n % (2 * across) == 0 else 1
+    return (n // (across * up), up, across)
+
+
+def gather_kernel(dims, w, out, send_sem, recv_sem, own_sem):
+    size_z, size_y, size_x = dims
+    me = lax.axis_index("seq")
+    x = lax.rem(me, size_x)
+    y = lax.rem(me // size_x, size_y)
+    z = me // (size_x * size_y)
+
+    def slot(dz, dy, dx):
+        return (
+            lax.rem(z + dz, size_z) * (size_y * size_x)
+            + lax.rem(y + dy, size_y) * size_x
+            + lax.rem(x + dx, size_x)
+        )
+
+    def held(dz, dy, dx):
+        return slot((size_z - dz) % size_z, (size_y - dy) % size_y, (size_x - dx) % size_x)
+
+    peers = [slot(d, 0, 0) for d in range(1, size_z)]
+    peers += [slot(0, d, 0) for d in range(1, size_y)]
+    peers += [slot(0, 0, d) for d in range(1, size_x)]
+    barrier = pltpu.get_barrier_semaphore()
+    for peer in peers:
+        pl.semaphore_signal(
+            barrier, inc=1, device_id={"seq": peer}, device_id_type=pl.DeviceIdType.MESH
+        )
+    pl.semaphore_wait(barrier, len(peers))
+
+    parts = w.shape[0] - 1
+    orders = ("zxy", "zyx")
+    copies = [{} for _ in range(parts)]
+
+    def send(part, item, axis, d):
+        step = dict(zip("zyx", item))
+        step[axis] = d
+        lands = (step["z"], step["y"], step["x"])
+        index = len(copies[part])
+        source = held(*item)
+        copy = pltpu.make_async_remote_copy(
+            src_ref=w.at[part + 1] if item == (0, 0, 0) else out.at[part, source],
+            dst_ref=out.at[part, source],
+            send_sem=send_sem.at[part, index],
+            recv_sem=recv_sem.at[part, index],
+            device_id={"seq": slot(*[d if a == axis else 0 for a in "zyx"])},
+            device_id_type=pl.DeviceIdType.MESH,
+        )
+        copy.start()
+        copies[part][lands] = copy
+
+    reach = {"z": size_z, "y": size_y, "x": size_x}
+
+    def spread(part, item, axis):
+        for d in range(1, reach[axis]):
+            send(part, item, axis, d)
+
+    own = [
+        pltpu.make_async_copy(w.at[part + 1], out.at[part, me], own_sem.at[part])
+        for part in range(parts)
+    ]
+    for part in range(parts):
+        spread(part, (0, 0, 0), "z")
+    for dz in range(size_z):
+        for part in range(parts):
+            if dz > 0:
+                copies[part][(dz, 0, 0)].wait_recv()
+            spread(part, (dz, 0, 0), orders[part][1])
+        for part in range(parts):
+            spread(part, (dz, 0, 0), orders[part][2])
+    for copy in own:
+        copy.start()
+    for dz in range(size_z):
+        for part in range(parts):
+            axis = orders[part][1]
+            for d in range(1, reach[axis]):
+                item = tuple(dz if a == "z" else d if a == axis else 0 for a in "zyx")
+                copies[part][item].wait_recv()
+                spread(part, item, orders[part][2])
+    for part in range(parts):
+        last = "zyx".index(orders[part][2])
+        for item, copy in copies[part].items():
+            copy.wait_send()
+            if item[last] > 0:
+                copy.wait_recv()
+    for copy in own:
+        copy.wait()
+
+
+def gathered_rows(weight):
+    n = lax.axis_size("seq")
+    three, rows, columns = weight.shape
+    out = pl.pallas_call(
+        functools.partial(gather_kernel, grid_of(n)),
+        in_specs=[pl.BlockSpec(memory_space=pl.ANY)],
+        out_specs=pl.BlockSpec(memory_space=pl.ANY),
+        out_shape=jax.ShapeDtypeStruct((three - 1, n, rows, columns), weight.dtype),
+        scratch_shapes=[
+            pltpu.SemaphoreType.DMA((three - 1, n - 1)),
+            pltpu.SemaphoreType.DMA((three - 1, n - 1)),
+            pltpu.SemaphoreType.DMA((three - 1,)),
+        ],
+        compiler_params=pltpu.CompilerParams(collective_id=0, has_side_effects=True),
+        name="gather_kv",
+    )(weight)
+    return out.reshape(three - 1, n * rows, columns)
 
 
 def gathered_features(spans):
@@ -140,14 +255,18 @@
     group = 2 if heads % 2 == 0 else heads
     wide = group * hd
 
-    weights = lax.all_gather(qkv_weight, "seq", axis=1, tiled=True)
+    key_value = gathered_rows(qkv_weight)
+    later, key_value = lax.optimization_barrier((qkv_weight[0], key_value))
+    query_weight = lax.all_gather(later, "seq", axis=0, tiled=True)
     spans = [tokens[0, :span]]
     for s in range(1, steps):
         spans.append(passed_along(tokens[0, s * span : (s + 1) * span], "seq", -s))
     features = gathered_features(spans)
-    q, k, v = [
-        jnp.dot(features, weights[c], preferred_element_type=f32).astype(bf16) for c in range(3)
+    k, v = [
+        jnp.dot(features, key_value[c], preferred_element_type=f32).astype(bf16)
+        for c in range(2)
     ]
+    q = jnp.dot(features, query_weight, preferred_element_type=f32).astype(bf16)
     rates = (
         rate_scale
         * jax.nn.softplus(jnp.dot(features, rate_weight, preferred_element_type=f32))
@@ -173,26 +292,24 @@
                 smem,
                 columns(total, g),
                 columns(total, g),
-                columns(total, g),
                 pl.BlockSpec((None, total, group), lambda i, g=g: (g, 0, 0)),
                 state(g),
                 state(g),
                 pl.BlockSpec((group, hd, three), lambda i, g=g: (g, 0, 0)),
             ],
             out_specs=[
-                pl.BlockSpec((total, wide), lambda i: (0, 0)),
+                pl.BlockSpec((steps, group, hd, three), lambda i: (0, 0, 0, 0)),
                 pl.BlockSpec((group, hd, three), lambda i: (0, 0, 0)),
                 pl.BlockSpec((group, hd, three), lambda i: (0, 0, 0)),
             ],
             out_shape=[
-                jax.ShapeDtypeStruct((total, wide), f32),
+                jax.ShapeDtypeStruct((steps, group, hd, three), bf16),
                 jax.ShapeDtypeStruct((group, hd, three), bf16),
                 jax.ShapeDtypeStruct((group, hd, three), bf16),
             ],
             compiler_params=params,
         )(
             begins,
-            q,
             k,
             v,
             rates.reshape(total, heads // group, group).transpose(1, 0, 2),
@@ -216,7 +333,7 @@
                     columns(total, g),
                     columns(window, g),
                     columns(window, g),
-                    pl.BlockSpec((total, wide), lambda i: (0, 0)),
+                    pl.BlockSpec((steps, group, hd, three), lambda i: (0, 0, 0, 0)),
                 ],
                 out_specs=pl.BlockSpec((total, wide), lambda i: (0, 0)),
                 out_shape=jax.ShapeDtypeStruct((total, wide), bf16),

time: 506 us -> 494 us (0.976)
  waiting for transfers between devices: 346 us -> 217 us
  Pallas kernels: 63.1 us -> 177 us
  matrix products: 36.9 us -> 42.8 us
    all_gather x1, waiting for transfers between devices: 121 us -> 0.01 us  [layer(): query_weight = lax.all_gather(later, 'seq', axis=0, tiled=True)]
    pallas_call x0 -> x1, Pallas kernels: none -> 104 us  [gathered_rows(): pl.pallas_call(functools.partial(gather_kernel, grid_of(n)), in_specs=[pl...]
    ppermute x8, waiting for transfers between devices: 224 us -> 217 us  [passed_along(): lax.ppermute(block, axis, [((i - distance) % n, i) for i in range(n)])]
    pallas_call x2, Pallas kernels: 34.6 us -> 42 us  [layer(): pl.pallas_call(functools.partial(fast_kernel, steps, span), grid=(1,), in...]
    dot_general x3, matrix products: 21.9 us -> 27.7 us  [the longest x2 18.3 us: layer(): jnp.dot(features, key_value[c], preferred_element_type=f32).astype(bf16)]
  transfers between devices with their start and end apart: 11 -> 11, of which waited for: 7 -> 6; matrix products, arithmetic and copies ran while one was open for 6% -> 9% of each run, Pallas kernels for 0% -> 9%
where the time goes in v1:
time: 494 us; the launch traced here: 488 us
  waiting for transfers between devices  217 us (44%)
  Pallas kernels  177 us (36%)
  matrix products  42.8 us (9%)
  local copies, waits for them, and re-layouts  14.6 us (3%)
  between operations  14.4 us (3%)
  other arithmetic  12.6 us (3%)
  starting transfers between devices  9.7 us (2%)
    ppermute x8, waiting for transfers between devices, passed_along(): lax.ppermute(block, axis, [((i - distance) % n, i) for i in range(n)])  217 us
    pallas_call x1, Pallas kernels, gathered_rows(): pl.pallas_call(functools.partial(gather_kernel, grid_of(n)), in_specs=[pl...  104 us
    pallas_call x2, Pallas kernels, layer(): pl.pallas_call(functools.partial(fast_kernel, steps, span), grid=(1,), in...  42 us
    pallas_call x2, Pallas kernels, layer(): pl.pallas_call(functools.partial(attend_kernel, steps, span, hd), grid=(1...  31.3 us
    dot_general x2, matrix products, layer(): jnp.dot(features, key_value[c], preferred_element_type=f32).astype(bf16)  18.3 us
    dot_general x2, matrix products, layer(): jnp.dot(part, out_weight, preferred_element_type=f32).astype(bf16)  13.4 us
  transfers between devices with their start and end apart: 11, of which 6 were waited for; matrix products, arithmetic and copies ran while one was open for 9% of the time, Pallas kernels for 9%

profile of v1, /device:TPU:0, one launch (start us, length us, event | category | flops | bytes accessed | tf_op | source)
XLA Modules:
  0.0 487.6 jit_solution(10897636681025193827)
XLA Ops:
  7.2 0.0 copy-start
  7.2 0.0 all-gather.2.cloned.1.call-start
  7.2 1.7 slice_bitcast_fusion.2
  8.9 103.7 %gather_kv.1 = bf16[2,16,192,768]{3,2,1,0:T(8,128)(2,1)} custom-call(bf16[3,192,768]{2,1,0:T(8,128)(2,1)} %w.1), custom_call_target="tpu_custom_call" | custom-call | tf_op jit(solution)/shard_map/gather_kv/pallas_call | solution.py:207
  112.6 0.0 copy-start.6
  112.6 0.0 all-gather.2.cloned.1.call-update
  112.7 0.0 reduce-scatter.3.cloned.1.call-start
  112.7 1.3 slice_bitcast_fusion
  114.1 9.3 %collective-permute-start.1 = (bf16[512,1536]{1,0:T(8,128)(2,1)S(1)}, bf16[512,1536]{1,0:T(8,128)(2,1)}, u32[]{:S(2)}, u32[]{:S(2)}) collective-permute-start(bf16[512,1536]{1,0:T(8,128)(2,1)S(1)} %get-tuple-element.19), channel_id=1, source_target_pairs={{2,0},{4,2},{6,4},{8,6},{10,8},{12,10},{14,12},{16,14},{18,16},{20... | collective-permute-start | bytes 4718600 | tf_op jit(solution)/shard_map/ppermute | solution.py:20
  123.4 38.5 %collective-permute-done.1 = bf16[512,1536]{1,0:T(8,128)(2,1)} collective-permute-done((bf16[512,1536]{1,0:T(8,128)(2,1)S(1)}, bf16[512,1536]{1,0:T(8,128)(2,1)}, u32[]{:S(2)}, u32[]{:S(2)}) %collective-permute-start.1) | collective-permute-done | bytes 1572896 | tf_op jit(solution)/shard_map/ppermute | solution.py:20
  161.9 0.6 constant_dynamic-slice_fusion
  162.5 2.0 pad_add_fusion.begins
  164.4 0.8 broadcast_in_dim.8
  165.2 0.2 constant_dynamic-update-slice_fusion.3
  165.4 1.6 constant_dynamic-update-slice_fusion.2
  167.0 1.6 constant_dynamic-update-slice_fusion.1
  168.6 1.6 constant_dynamic-update-slice_fusion
  170.3 2.7 copy-done.2
  173.0 1.7 fusion.16
  174.7 0.0 slice-start
  174.8 1.3 copy.13
  176.1 9.5 %fusion.6.k = bf16[1024,768]{1,0:T(8,128)(2,1)} fusion(bf16[1024,3072]{1,0:T(8,128)(2,1)} %copy-done.2, bf16[2,3072,768]{2,1,0:T(8,128)(2,1)} %bitcast.49), kind=kOutput, calls=%fused_computation.11 | convolution fusion | flops 4832624640 | bytes 12582912 | tf_op jit(solution)/shard_map/dot_general | solution.py:266
  185.7 8.7 %fusion.9.v = bf16[1024,768]{1,0:T(8,128)(2,1)} fusion(bf16[1024,3072]{1,0:T(8,128)(2,1)S(1)} %bitcast.42, bf16[2,3072,768]{2,1,0:T(8,128)(2,1)} %bitcast.50), kind=kOutput, calls=%fused_computation.12 | convolution fusion | flops 4832624640 | bytes 12582912 | tf_op jit(solution)/shard_map/dot_general | solution.py:266
  194.4 14.8 %shard_map.123 = (bf16[2,2,192,2304]{3,2,1,0:T(8,128)(2,1)}, bf16[2,192,2304]{2,1,0:T(8,128)(2,1)}, bf16[2,192,2304]{2,1,0:T(8,128)(2,1)}) custom-call(s32[2]{0:T(128)} %pad_add_fusion.begins, bf16[1024,768]{1,0:T(8,128)(2,1)} %fusion.6.k, bf16[1024,768]{1,0:T(8,128)(2,1)} %fusion.9.v, f32[2,1024,2]{2,1,0:T(8,128)} %bitcast.47, f32[1,4,192,2304]{3,2,1,0:T(8,128)} %fast.3, ...), custom_call_target="tpu_custom_call" | custom-call | tf_op jit(solution)/shard_map/pallas_call | solution.py:288
  209.2 27.2 %shard_map.121 = (bf16[2,2,192,2304]{3,2,1,0:T(8,128)(2,1)}, bf16[2,192,2304]{2,1,0:T(8,128)(2,1)}, bf16[2,192,2304]{2,1,0:T(8,128)(2,1)}) custom-call(s32[2]{0:T(128)} %pad_add_fusion.begins, bf16[1024,768]{1,0:T(8,128)(2,1)} %fusion.6.k, bf16[1024,768]{1,0:T(8,128)(2,1)} %fusion.9.v, f32[2,1024,2]{2,1,0:T(8,128)} %bitcast.48, f32[1,4,192,2304]{3,2,1,0:T(8,128)} %fast.3, ...), custom_call_target="tpu_custom_call" | custom-call | tf_op jit(solution)/shard_map/pallas_call | solution.py:288
  236.4 9.4 %convolution_convert_fusion.2.q = bf16[1024,768]{1,0:T(8,128)(2,1)} fusion(bf16[1024,3072]{1,0:T(8,128)(2,1)} %copy-done.2, bf16[3072,768]{1,0:T(8,128)(2,1)} %all-gather.2.cloned.1.call-done), kind=kOutput, calls=%fused_computation.13 | convolution fusion | flops 4832624640 | bytes 12582912 | tf_op jit(solution)/shard_map/dot_general | solution.py:269
  245.8 15.5 %shard_map.124 = bf16[1024,384]{1,0:T(8,128)(2,1)} custom-call(s32[2]{0:T(128)} %pad_add_fusion.begins, bf16[1024,768]{1,0:T(8,128)(2,1)} %convolution_convert_fusion.2.q, bf16[1024,768]{1,0:T(8,128)(2,1)} %fusion.6.k, bf16[1024,768]{1,0:T(8,128)(2,1)} %fusion.9.v, bf16[2048,768]{1,0:T(8,128)(2,1)} %bitcast.43, bf16[2048,768]{1,0:T(8,128)(2,1)} %bitcast.45, ...), custom_call_target="tpu_custom_call" | custom-call | tf_op jit(solution)/shard_map/pallas_call | solution.py:326
  261.3 15.8 %shard_map.122 = bf16[1024,384]{1,0:T(8,128)(2,1)} custom-call(s32[2]{0:T(128)} %pad_add_fusion.begins, bf16[1024,768]{1,0:T(8,128)(2,1)} %convolution_convert_fusion.2.q, bf16[1024,768]{1,0:T(8,128)(2,1)} %fusion.6.k, bf16[1024,768]{1,0:T(8,128)(2,1)} %fusion.9.v, bf16[2048,768]{1,0:T(8,128)(2,1)} %bitcast.44, bf16[2048,768]{1,0:T(8,128)(2,1)} %bitcast.46, ...), custom_call_target="tpu_custom_call" | custom-call | tf_op jit(solution)/shard_map/pallas_call | solution.py:326
  277.1 6.8 %convolution_convert_fusion.1 = bf16[512,3072]{1,0:T(8,128)(2,1)} fusion(bf16[768,3072]{1,0:T(8,128)(2,1)} %param.18, bf16[1024,384]{1,0:T(8,128)(2,1)} %shard_map.122, bf16[1024,384]{1,0:T(8,128)(2,1)S(1)} %copy-done.4), kind=kOutput, calls=%fused_computation.7 | convolution fusion | flops 2419064832 | bytes 9437184 | tf_op jit(solution)/shard_map/dot_general | solution.py:349
  283.8 0.0 reduce-scatter.3.cloned.1.call-update
  283.9 0.0 reduce-scatter.5.cloned.1.call-start
  283.9 1.1 copy-done.5
  285.0 0.1 pad_maximum_fusion
  285.0 0.1 collective-permute-start.3
  285.1 23.8 %collective-permute-done.3 = bf16[512,768]{1,0:T(8,128)(2,1)S(1)} collective-permute-done((bf16[512,768]{1,0:T(8,128)(2,1)S(1)}, bf16[512,768]{1,0:T(8,128)(2,1)S(1)}, u32[]{:S(2)}, u32[]{:S(2)}) %collective-permute-start.3) | collective-permute-done | bytes 786464 | tf_op jit(solution)/shard_map/ppermute | solution.py:20
  308.9 6.7 %convolution_convert_fusion = bf16[512,3072]{1,0:T(8,128)(2,1)} fusion(bf16[512,768]{1,0:T(8,128)(2,1)S(1)} %collective-permute-done.3, bf16[768,3072]{1,0:T(8,128)(2,1)} %param.18), kind=kOutput, calls=%fused_computation.6 | convolution fusion | flops 2417491968 | bytes 8650752 | tf_op jit(solution)/shard_map/dot_general | solution.py:349
  315.6 0.0 reduce-scatter.5.cloned.1.call-update
  315.6 0.1 collective-permute-start.5
  315.7 0.1 collective-permute-start.4
  315.7 0.1 collective-permute-start.7
  315.8 0.1 collective-permute-start.6
  315.9 45.1 %collective-permute-done.5 = bf16[2,192,2304]{2,1,0:T(8,128)(2,1)S(1)} collective-permute-done((bf16[2,192,2304]{2,1,0:T(8,128)(2,1)}, bf16[2,192,2304]{2,1,0:T(8,128)(2,1)S(1)}, u32[]{:S(2)}, u32[]{:S(2)}) %collective-permute-start.5) | collective-permute-done | bytes 1769504 | tf_op jit(solution)/shard_map/ppermute | solution.py:20
  360.9 37.9 %collective-permute-done.4 = bf16[2,192,2304]{2,1,0:T(8,128)(2,1)S(1)} collective-permute-done((bf16[2,192,2304]{2,1,0:T(8,128)(2,1)}, bf16[2,192,2304]{2,1,0:T(8,128)(2,1)S(1)}, u32[]{:S(2)}, u32[]{:S(2)}) %collective-permute-start.4) | collective-permute-done | bytes 1769504 | tf_op jit(solution)/shard_map/ppermute | solution.py:20
  398.9 3.4 maximum_convert_fusion
  402.3 34.5 %collective-permute-done.7 = bf16[2,192,2304]{2,1,0:T(8,128)(2,1)S(1)} collective-permute-done((bf16[2,192,2304]{2,1,0:T(8,128)(2,1)S(1)}, bf16[2,192,2304]{2,1,0:T(8,128)(2,1)S(1)}, u32[]{:S(2)}, u32[]{:S(2)}) %collective-permute-start.7) | collective-permute-done | bytes 1769504 | tf_op jit(solution)/shard_map/ppermute | solution.py:20
  436.8 36.7 %collective-permute-done.6 = bf16[2,192,2304]{2,1,0:T(8,128)(2,1)S(1)} collective-permute-done((bf16[2,192,2304]{2,1,0:T(8,128)(2,1)}, bf16[2,192,2304]{2,1,0:T(8,128)(2,1)S(1)}, u32[]{:S(2)}, u32[]{:S(2)}) %collective-permute-start.6) | collective-permute-done | bytes 1769504 | tf_op jit(solution)/shard_map/ppermute | solution.py:20
  473.5 3.4 maximum_convert_fusion.1
  476.9 3.7 maximum_bitcast_fusion
  (24 shorter events, 0.1 us)
Async XLA Ops:
  7.2 165.8 %copy-start = (bf16[3072,4]{0,1:T(4,128)(2,1)S(1)}, bf16[3072,4]{0,1:T(4,128)(2,1)}, u32[]{:S(2)}) copy-start(bf16[3072,4]{0,1:T(4,128)(2,1)} %param.17) | copy-start | bytes 73732
  7.2 229.2 %all-gather.2.cloned.1.call-start = ((), (), s32[]{:S(2)}) async-start(), calls=%async_computation.2 | async-start | bytes 5013504 | tf_op jit(solution)/shard_map/all_gather | solution.py:260
  8.9 103.8 %copy-start.3 = (bf16[1,1024,1536]{2,1,0:T(8,128)(2,1)S(1)}, bf16[1,1024,1536]{2,1,0:T(8,128)(2,1)}, u32[]{:S(2)}) copy-start(bf16[1,1024,1536]{2,1,0:T(8,128)(2,1)} %param.10) | copy-start | bytes 9437188
  112.6 49.3 %copy-start.6 = (s32[2,16]{1,0:T(2,128)S(1)}, s32[2,16]{1,0:T(2,128)}, u32[]{:S(2)}) copy-start(s32[2,16]{1,0:T(2,128)} %param.19) | copy-start | bytes 388
  112.7 364.2 %reduce-scatter.3.cloned.1.call-start = ((), (), s32[]{:S(2)}) async-start(), calls=%async_computation.3 | async-start | bytes 4718592 | tf_op jit(solution)/shard_map/reduce_scatter | solution.py:351
  114.1 47.8 %collective-permute-start.1 = (bf16[512,1536]{1,0:T(8,128)(2,1)S(1)}, bf16[512,1536]{1,0:T(8,128)(2,1)}, u32[]{:S(2)}, u32[]{:S(2)}) collective-permute-start(bf16[512,1536]{1,0:T(8,128)(2,1)S(1)} %get-tuple-element.19), channel_id=1, source_target_pairs={{2,0},{4,2},{6,4},{8,6},{10,8},{12,10},{14,12},{16,14},{18,16},{20... | collective-permute-start | bytes 4718600 | tf_op jit(solution)/shard_map/ppermute | solution.py:20
  123.4 42.1 %collective-permute-start = (bf16[512,1536]{1,0:T(8,128)(2,1)}, bf16[512,1536]{1,0:T(8,128)(2,1)}, u32[]{:S(2)}, u32[]{:S(2)}) collective-permute-start(bf16[512,1536]{1,0:T(8,128)(2,1)} %get-tuple-element.20), channel_id=1, source_target_pairs={{1,0},{0,1},{3,2},{2,3},{5,4},{4,5},{7,6},{6,7},{9,8},{8,9},{11,10... | collective-permute-start | bytes 4718600 | tf_op jit(solution)/shard_map/ppermute | solution.py:20
  161.9 6.7 %collective-permute-start.2 = (bf16[512,1536]{1,0:T(8,128)(2,1)}, bf16[512,1536]{1,0:T(8,128)(2,1)}, u32[]{:S(2)}, u32[]{:S(2)}) collective-permute-start(bf16[512,1536]{1,0:T(8,128)(2,1)} %collective-permute-done.1), channel_id=1, source_target_pairs={{1,0},{0,1},{3,2},{2,3},{5,4},{4,5},{7,6},{6,7},{9,8},{8,9},{11,10... | collective-permute-start | bytes 4718600 | tf_op jit(solution)/shard_map/ppermute | solution.py:20
  170.3 2.7 copy-start.2
  174.7 10.9 %slice-start = ((s8[6291456]{0:T(1024)(128)(4,1)}), s8[2097152]{0:T(1024)(128)(4,1)S(1)}, s32[]{:S(2)}) async-start(s8[6291456]{0:T(1024)(128)(4,1)} %bitcast.41), calls=%async_computation.5 | async-start | bytes 4194304
  176.1 9.6 %slice-start.1 = ((s8[6291456]{0:T(1024)(128)(4,1)}), s8[4194304]{0:T(1024)(128)(4,1)S(1)}, s32[]{:S(2)}) async-start(s8[6291456]{0:T(1024)(128)(4,1)} %bitcast.41), calls=%async_computation.6 | async-start | bytes 8388608
  261.3 15.8 %copy-start.4 = (bf16[1024,384]{1,0:T(8,128)(2,1)S(1)}, bf16[1024,384]{1,0:T(8,128)(2,1)}, u32[]{:S(2)}) copy-start(bf16[1024,384]{1,0:T(8,128)(2,1)} %shard_map.124) | copy-start | bytes 2359300
  283.8 1.1 copy-start.5
  283.9 193.0 %reduce-scatter.5.cloned.1.call-start = ((), (), s32[]{:S(2)}) async-start(), calls=%async_computation.4 | async-start | bytes 4718592 | tf_op jit(solution)/shard_map/reduce_scatter | solution.py:351
  285.0 30.7 %copy-start.7 = (bf16[2,192,2304]{2,1,0:T(8,128)(2,1)S(1)}, bf16[2,192,2304]{2,1,0:T(8,128)(2,1)}, u32[]{:S(2)}) copy-start(bf16[2,192,2304]{2,1,0:T(8,128)(2,1)} %get-tuple-element.18) | copy-start | bytes 5308420
  285.0 23.9 %collective-permute-start.3 = (bf16[512,768]{1,0:T(8,128)(2,1)S(1)}, bf16[512,768]{1,0:T(8,128)(2,1)S(1)}, u32[]{:S(2)}, u32[]{:S(2)}) collective-permute-start(bf16[512,768]{1,0:T(8,128)(2,1)S(1)} %pad_maximum_fusion), channel_id=1, source_target_pairs={{30,0},{0,2},{2,4},{4,6},{6,8},{8,10},{10,12},{12,14},{14,16},{16,... | collective-permute-start | bytes 2359304 | tf_op jit(solution)/shard_map/ppermute | solution.py:20
  315.6 45.3 %collective-permute-start.5 = (bf16[2,192,2304]{2,1,0:T(8,128)(2,1)}, bf16[2,192,2304]{2,1,0:T(8,128)(2,1)S(1)}, u32[]{:S(2)}, u32[]{:S(2)}) collective-permute-start(bf16[2,192,2304]{2,1,0:T(8,128)(2,1)} %get-tuple-element.16), channel_id=1, source_target_pairs={{30,0},{0,2},{2,4},{4,6},{6,8},{8,10},{10,12},{12,14},{14,16},{16,... | collective-permute-start | bytes 5308424 | tf_op jit(solution)/shard_map/ppermute | solution.py:20
  315.7 83.2 %collective-permute-start.4 = (bf16[2,192,2304]{2,1,0:T(8,128)(2,1)}, bf16[2,192,2304]{2,1,0:T(8,128)(2,1)S(1)}, u32[]{:S(2)}, u32[]{:S(2)}) collective-permute-start(bf16[2,192,2304]{2,1,0:T(8,128)(2,1)} %get-tuple-element.15), channel_id=1, source_target_pairs={{30,0},{0,2},{2,4},{4,6},{6,8},{8,10},{10,12},{12,14},{14,16},{16,... | collective-permute-start | bytes 5308424 | tf_op jit(solution)/shard_map/ppermute | solution.py:20
  315.7 121.0 %collective-permute-start.7 = (bf16[2,192,2304]{2,1,0:T(8,128)(2,1)S(1)}, bf16[2,192,2304]{2,1,0:T(8,128)(2,1)S(1)}, u32[]{:S(2)}, u32[]{:S(2)}) collective-permute-start(bf16[2,192,2304]{2,1,0:T(8,128)(2,1)S(1)} %copy-done.7), channel_id=1, source_target_pairs={{30,0},{0,2},{2,4},{4,6},{6,8},{8,10},{10,12},{12,14},{14,16},{16,... | collective-permute-start | bytes 5308424 | tf_op jit(solution)/shard_map/ppermute | solution.py:20
  315.8 157.7 %collective-permute-start.6 = (bf16[2,192,2304]{2,1,0:T(8,128)(2,1)}, bf16[2,192,2304]{2,1,0:T(8,128)(2,1)S(1)}, u32[]{:S(2)}, u32[]{:S(2)}) collective-permute-start(bf16[2,192,2304]{2,1,0:T(8,128)(2,1)} %get-tuple-element.17), channel_id=1, source_target_pairs={{30,0},{0,2},{2,4},{4,6},{6,8},{8,10},{10,12},{12,14},{14,16},{16,... | collective-permute-start | bytes 5308424 | tf_op jit(solution)/shard_map/ppermute | solution.py:20
  473.5 7.2 %copy-start.1 = (bf16[3072,4]{0,1:T(4,128)(2,1)S(1)}, bf16[3072,4]{0,1:T(4,128)(2,1)}, u32[]{:S(2)}) copy-start(bf16[3072,4]{0,1:T(4,128)(2,1)} %param.17) | copy-start | bytes 73732
Sparse Core Ops, SparseCore 0:
  112.8 113.2 all-gather.1
  284.0 15.0 reduce-scatter.2
  315.7 11.0 reduce-scatter.4

commit v2 on v1

--- a/solution.py
+++ b/solution.py
@@ -266,7 +266,6 @@
         jnp.dot(features, key_value[c], preferred_element_type=f32).astype(bf16)
         for c in range(2)
     ]
-    q = jnp.dot(features, query_weight, preferred_element_type=f32).astype(bf16)
     rates = (
         rate_scale
         * jax.nn.softplus(jnp.dot(features, rate_weight, preferred_element_type=f32))
@@ -284,6 +283,7 @@
     params = pltpu.CompilerParams(vmem_limit_bytes=58 * 1024 * 1024)
     applied = []
     sent = []
+    kept = []
     for g in range(heads // group):
         a, w, m = pl.pallas_call(
             functools.partial(fast_kernel, steps, span),
@@ -318,8 +318,11 @@
             init_fast,
         )
         applied.append(a)
-        sent.append((passed_along(w, "seq", steps - 1), passed_along(m, "seq", steps - 1)))
-
+        w, query_weight = lax.optimization_barrier((w, query_weight))
+        sent.append(passed_along(w, "seq", steps - 1))
+        kept.append(m)
+
+    q = jnp.dot(features, query_weight, preferred_element_type=f32).astype(bf16)
     mixes = []
     for g in range(heads // group):
         mixes.append(
@@ -344,6 +347,8 @@
     placed = [mix[:span]]
     for s in range(1, steps):
         placed.append(passed_along(mix[s * span : (s + 1) * span], "seq", s))
+    *kept, placed[-1] = lax.optimization_barrier((*kept, placed[-1]))
+    moved = [passed_along(m, "seq", steps - 1) for m in kept]
     reduced = []
     for part in placed:
         partial_value = jnp.dot(part, out_weight, preferred_element_type=f32).astype(bf16)
@@ -351,8 +356,8 @@
             lax.psum_scatter(partial_value, "head", scatter_dimension=1, tiled=True)
         )
     mixed = jnp.concatenate(reduced, axis=0)
-    fast_out = jnp.concatenate([w for w, _ in sent], axis=0).astype(f32)
-    mom_out = jnp.concatenate([m for _, m in sent], axis=0).astype(f32)
+    fast_out = jnp.concatenate(sent, axis=0).astype(f32)
+    mom_out = jnp.concatenate(moved, axis=0).astype(f32)
     return (mixed[None], fast_out[None], mom_out[None])
 
 

time: 494 us -> 494 us (level)
  no operation moved by 1% of the time
where the time goes in v2:
time: 494 us; the launch traced here: 488 us
  waiting for transfers between devices  217 us (44%)
  Pallas kernels  177 us (36%)
  matrix products  42.9 us (9%)
  local copies, waits for them, and re-layouts  14.6 us (3%)
  between operations  14.4 us (3%)
  other arithmetic  12.6 us (3%)
  starting transfers between devices  9.7 us (2%)
    ppermute x8, waiting for transfers between devices, passed_along(): lax.ppermute(block, axis, [((i - distance) % n, i) for i in range(n)])  217 us
    pallas_call x1, Pallas kernels, gathered_rows(): pl.pallas_call(functools.partial(gather_kernel, grid_of(n)), in_specs=[pl...  104 us
    pallas_call x2, Pallas kernels, layer(): pl.pallas_call(functools.partial(fast_kernel, steps, span), grid=(1,), in...  42 us
    pallas_call x2, Pallas kernels, layer(): pl.pallas_call(functools.partial(attend_kernel, steps, span, hd), grid=(1...  31.3 us
    dot_general x2, matrix products, layer(): jnp.dot(features, key_value[c], preferred_element_type=f32).astype(bf16)  18.3 us
    dot_general x2, matrix products, layer(): jnp.dot(part, out_weight, preferred_element_type=f32).astype(bf16)  13.5 us
  transfers between devices with their start and end apart: 11, of which 6 were waited for; matrix products, arithmetic and copies ran while one was open for 9% of the time, Pallas kernels for 9%

profile of v2, /device:TPU:0, one launch (start us, length us, event | category | flops | bytes accessed | tf_op | source)
XLA Modules:
  0.0 487.7 jit_solution(15207253937668092914)
XLA Ops:
  7.2 0.0 copy-start
  7.2 0.0 all-gather.2.cloned.1.call-start
  7.2 1.7 slice_bitcast_fusion.2
  8.9 103.7 %gather_kv.1 = bf16[2,16,192,768]{3,2,1,0:T(8,128)(2,1)} custom-call(bf16[3,192,768]{2,1,0:T(8,128)(2,1)} %w.1), custom_call_target="tpu_custom_call" | custom-call | tf_op jit(solution)/shard_map/gather_kv/pallas_call | solution.py:207
  112.6 0.0 copy-start.6
  112.6 0.0 all-gather.2.cloned.1.call-update
  112.7 0.0 reduce-scatter.3.cloned.1.call-start
  112.7 1.3 slice_bitcast_fusion
  114.1 9.3 %collective-permute-start.1 = (bf16[512,1536]{1,0:T(8,128)(2,1)S(1)}, bf16[512,1536]{1,0:T(8,128)(2,1)}, u32[]{:S(2)}, u32[]{:S(2)}) collective-permute-start(bf16[512,1536]{1,0:T(8,128)(2,1)S(1)} %get-tuple-element.33), channel_id=1, source_target_pairs={{2,0},{4,2},{6,4},{8,6},{10,8},{12,10},{14,12},{16,14},{18,16},{20... | collective-permute-start | bytes 4718600 | tf_op jit(solution)/shard_map/ppermute | solution.py:20
  123.4 38.5 %collective-permute-done.1 = bf16[512,1536]{1,0:T(8,128)(2,1)} collective-permute-done((bf16[512,1536]{1,0:T(8,128)(2,1)S(1)}, bf16[512,1536]{1,0:T(8,128)(2,1)}, u32[]{:S(2)}, u32[]{:S(2)}) %collective-permute-start.1) | collective-permute-done | bytes 1572896 | tf_op jit(solution)/shard_map/ppermute | solution.py:20
  161.9 0.6 constant_dynamic-slice_fusion
  162.5 2.0 pad_add_fusion.begins
  164.4 0.8 broadcast_in_dim.8
  165.2 0.2 constant_dynamic-update-slice_fusion.3
  165.4 1.6 constant_dynamic-update-slice_fusion.2
  167.0 1.6 constant_dynamic-update-slice_fusion.1
  168.6 1.6 constant_dynamic-update-slice_fusion
  170.3 2.7 copy-done.2
  173.0 1.7 fusion.16
  174.7 0.0 slice-start
  174.8 1.3 copy.13
  176.1 9.5 %fusion.9.v = bf16[1024,768]{1,0:T(8,128)(2,1)} fusion(bf16[1024,3072]{1,0:T(8,128)(2,1)} %copy-done.2, bf16[2,3072,768]{2,1,0:T(8,128)(2,1)} %bitcast.49), kind=kOutput, calls=%fused_computation.12 | convolution fusion | flops 4832624640 | bytes 12582912 | tf_op jit(solution)/shard_map/dot_general | solution.py:266
  185.7 8.7 %fusion.6.k = bf16[1024,768]{1,0:T(8,128)(2,1)} fusion(bf16[1024,3072]{1,0:T(8,128)(2,1)S(1)} %bitcast.42, bf16[2,3072,768]{2,1,0:T(8,128)(2,1)} %bitcast.50), kind=kOutput, calls=%fused_computation.11 | convolution fusion | flops 4832624640 | bytes 12582912 | tf_op jit(solution)/shard_map/dot_general | solution.py:266
  194.4 14.8 %shard_map.122 = (bf16[2,2,192,2304]{3,2,1,0:T(8,128)(2,1)}, bf16[2,192,2304]{2,1,0:T(8,128)(2,1)}, bf16[2,192,2304]{2,1,0:T(8,128)(2,1)}) custom-call(s32[2]{0:T(128)} %pad_add_fusion.begins, bf16[1024,768]{1,0:T(8,128)(2,1)} %fusion.6.k, bf16[1024,768]{1,0:T(8,128)(2,1)} %fusion.9.v, f32[2,1024,2]{2,1,0:T(8,128)} %bitcast.47, f32[1,4,192,2304]{3,2,1,0:T(8,128)} %fast.3, ...), custom_call_target="tpu_custom_call" | custom-call | tf_op jit(solution)/shard_map/pallas_call | solution.py:288
  209.2 27.2 %shard_map.121 = (bf16[2,2,192,2304]{3,2,1,0:T(8,128)(2,1)}, bf16[2,192,2304]{2,1,0:T(8,128)(2,1)}, bf16[2,192,2304]{2,1,0:T(8,128)(2,1)}) custom-call(s32[2]{0:T(128)} %pad_add_fusion.begins, bf16[1024,768]{1,0:T(8,128)(2,1)} %fusion.6.k, bf16[1024,768]{1,0:T(8,128)(2,1)} %fusion.9.v, f32[2,1024,2]{2,1,0:T(8,128)} %bitcast.48, f32[1,4,192,2304]{3,2,1,0:T(8,128)} %fast.3, ...), custom_call_target="tpu_custom_call" | custom-call | tf_op jit(solution)/shard_map/pallas_call | solution.py:288
  236.4 9.4 %convolution_convert_fusion.2.q = bf16[1024,768]{1,0:T(8,128)(2,1)} fusion(bf16[1024,3072]{1,0:T(8,128)(2,1)} %copy-done.2, bf16[3072,768]{1,0:T(8,128)(2,1)} %all-gather.2.cloned.1.call-done), kind=kOutput, calls=%fused_computation.13 | convolution fusion | flops 4832624640 | bytes 12582912 | tf_op jit(solution)/shard_map/dot_general | solution.py:325
  245.8 15.5 %shard_map.124 = bf16[1024,384]{1,0:T(8,128)(2,1)} custom-call(s32[2]{0:T(128)} %pad_add_fusion.begins, bf16[1024,768]{1,0:T(8,128)(2,1)} %convolution_convert_fusion.2.q, bf16[1024,768]{1,0:T(8,128)(2,1)} %fusion.6.k, bf16[1024,768]{1,0:T(8,128)(2,1)} %fusion.9.v, bf16[2048,768]{1,0:T(8,128)(2,1)} %bitcast.43, bf16[2048,768]{1,0:T(8,128)(2,1)} %bitcast.45, ...), custom_call_target="tpu_custom_call" | custom-call | tf_op jit(solution)/shard_map/pallas_call | solution.py:329
  261.3 15.8 %shard_map.123 = bf16[1024,384]{1,0:T(8,128)(2,1)} custom-call(s32[2]{0:T(128)} %pad_add_fusion.begins, bf16[1024,768]{1,0:T(8,128)(2,1)} %convolution_convert_fusion.2.q, bf16[1024,768]{1,0:T(8,128)(2,1)} %fusion.6.k, bf16[1024,768]{1,0:T(8,128)(2,1)} %fusion.9.v, bf16[2048,768]{1,0:T(8,128)(2,1)} %bitcast.44, bf16[2048,768]{1,0:T(8,128)(2,1)} %bitcast.46, ...), custom_call_target="tpu_custom_call" | custom-call | tf_op jit(solution)/shard_map/pallas_call | solution.py:329
  277.1 6.8 %convolution_convert_fusion.1 = bf16[512,3072]{1,0:T(8,128)(2,1)} fusion(bf16[768,3072]{1,0:T(8,128)(2,1)} %param.18, bf16[1024,384]{1,0:T(8,128)(2,1)} %shard_map.123, bf16[1024,384]{1,0:T(8,128)(2,1)S(1)} %copy-done.4), kind=kOutput, calls=%fused_computation.7 | convolution fusion | flops 2419064832 | bytes 9437184 | tf_op jit(solution)/shard_map/dot_general | solution.py:354
  283.8 0.0 reduce-scatter.3.cloned.1.call-update
  283.9 0.0 reduce-scatter.5.cloned.1.call-start
  283.9 1.1 copy-done.5
  285.0 0.1 pad_maximum_fusion
  285.0 0.1 collective-permute-start.3
  285.1 23.8 %collective-permute-done.3 = bf16[512,768]{1,0:T(8,128)(2,1)S(1)} collective-permute-done((bf16[512,768]{1,0:T(8,128)(2,1)S(1)}, bf16[512,768]{1,0:T(8,128)(2,1)S(1)}, u32[]{:S(2)}, u32[]{:S(2)}) %collective-permute-start.3) | collective-permute-done | bytes 786464 | tf_op jit(solution)/shard_map/ppermute | solution.py:20
  308.9 6.8 %convolution_convert_fusion = bf16[512,3072]{1,0:T(8,128)(2,1)} fusion(bf16[512,768]{1,0:T(8,128)(2,1)S(1)} %collective-permute-done.3, bf16[768,3072]{1,0:T(8,128)(2,1)} %param.18), kind=kOutput, calls=%fused_computation.6 | convolution fusion | flops 2417491968 | bytes 8650752 | tf_op jit(solution)/shard_map/dot_general | solution.py:354
  315.7 0.0 reduce-scatter.5.cloned.1.call-update
  315.7 0.1 collective-permute-start.4
  315.8 0.1 collective-permute-start.5
  315.9 0.1 collective-permute-start.6
  315.9 0.1 collective-permute-start.7
  316.0 45.1 %collective-permute-done.4 = bf16[2,192,2304]{2,1,0:T(8,128)(2,1)S(1)} collective-permute-done((bf16[2,192,2304]{2,1,0:T(8,128)(2,1)}, bf16[2,192,2304]{2,1,0:T(8,128)(2,1)S(1)}, u32[]{:S(2)}, u32[]{:S(2)}) %collective-permute-start.4) | collective-permute-done | bytes 1769504 | tf_op jit(solution)/shard_map/ppermute | solution.py:20
  361.1 37.9 %collective-permute-done.5 = bf16[2,192,2304]{2,1,0:T(8,128)(2,1)S(1)} collective-permute-done((bf16[2,192,2304]{2,1,0:T(8,128)(2,1)}, bf16[2,192,2304]{2,1,0:T(8,128)(2,1)S(1)}, u32[]{:S(2)}, u32[]{:S(2)}) %collective-permute-start.5) | collective-permute-done | bytes 1769504 | tf_op jit(solution)/shard_map/ppermute | solution.py:20
  399.0 3.4 maximum_convert_fusion
  402.4 34.5 %collective-permute-done.6 = bf16[2,192,2304]{2,1,0:T(8,128)(2,1)S(1)} collective-permute-done((bf16[2,192,2304]{2,1,0:T(8,128)(2,1)S(1)}, bf16[2,192,2304]{2,1,0:T(8,128)(2,1)S(1)}, u32[]{:S(2)}, u32[]{:S(2)}) %collective-permute-start.6) | collective-permute-done | bytes 1769504 | tf_op jit(solution)/shard_map/ppermute | solution.py:20
  436.9 36.7 %collective-permute-done.7 = bf16[2,192,2304]{2,1,0:T(8,128)(2,1)S(1)} collective-permute-done((bf16[2,192,2304]{2,1,0:T(8,128)(2,1)}, bf16[2,192,2304]{2,1,0:T(8,128)(2,1)S(1)}, u32[]{:S(2)}, u32[]{:S(2)}) %collective-permute-start.7) | collective-permute-done | bytes 1769504 | tf_op jit(solution)/shard_map/ppermute | solution.py:20
  473.6 3.4 maximum_convert_fusion.1
  477.0 3.7 maximum_bitcast_fusion
  (24 shorter events, 0.1 us)
Async XLA Ops:
  7.2 165.8 %copy-start = (bf16[3072,4]{0,1:T(4,128)(2,1)S(1)}, bf16[3072,4]{0,1:T(4,128)(2,1)}, u32[]{:S(2)}) copy-start(bf16[3072,4]{0,1:T(4,128)(2,1)} %param.17) | copy-start | bytes 73732
  7.2 229.2 %all-gather.2.cloned.1.call-start = ((), (), s32[]{:S(2)}) async-start(), calls=%async_computation.2 | async-start | bytes 5013504 | tf_op jit(solution)/shard_map/all_gather | solution.py:260
  8.9 103.8 %copy-start.3 = (bf16[1,1024,1536]{2,1,0:T(8,128)(2,1)S(1)}, bf16[1,1024,1536]{2,1,0:T(8,128)(2,1)}, u32[]{:S(2)}) copy-start(bf16[1,1024,1536]{2,1,0:T(8,128)(2,1)} %param.10) | copy-start | bytes 9437188
  112.6 49.3 %copy-start.6 = (s32[2,16]{1,0:T(2,128)S(1)}, s32[2,16]{1,0:T(2,128)}, u32[]{:S(2)}) copy-start(s32[2,16]{1,0:T(2,128)} %param.19) | copy-start | bytes 388
  112.7 364.4 %reduce-scatter.3.cloned.1.call-start = ((), (), s32[]{:S(2)}) async-start(), calls=%async_computation.3 | async-start | bytes 4718592 | tf_op jit(solution)/shard_map/reduce_scatter | solution.py:356
  114.1 47.8 %collective-permute-start.1 = (bf16[512,1536]{1,0:T(8,128)(2,1)S(1)}, bf16[512,1536]{1,0:T(8,128)(2,1)}, u32[]{:S(2)}, u32[]{:S(2)}) collective-permute-start(bf16[512,1536]{1,0:T(8,128)(2,1)S(1)} %get-tuple-element.33), channel_id=1, source_target_pairs={{2,0},{4,2},{6,4},{8,6},{10,8},{12,10},{14,12},{16,14},{18,16},{20... | collective-permute-start | bytes 4718600 | tf_op jit(solution)/shard_map/ppermute | solution.py:20
  123.4 42.1 %collective-permute-start = (bf16[512,1536]{1,0:T(8,128)(2,1)}, bf16[512,1536]{1,0:T(8,128)(2,1)}, u32[]{:S(2)}, u32[]{:S(2)}) collective-permute-start(bf16[512,1536]{1,0:T(8,128)(2,1)} %get-tuple-element.34), channel_id=1, source_target_pairs={{1,0},{0,1},{3,2},{2,3},{5,4},{4,5},{7,6},{6,7},{9,8},{8,9},{11,10... | collective-permute-start | bytes 4718600 | tf_op jit(solution)/shard_map/ppermute | solution.py:20
  161.9 6.7 %collective-permute-start.2 = (bf16[512,1536]{1,0:T(8,128)(2,1)}, bf16[512,1536]{1,0:T(8,128)(2,1)}, u32[]{:S(2)}, u32[]{:S(2)}) collective-permute-start(bf16[512,1536]{1,0:T(8,128)(2,1)} %collective-permute-done.1), channel_id=1, source_target_pairs={{1,0},{0,1},{3,2},{2,3},{5,4},{4,5},{7,6},{6,7},{9,8},{8,9},{11,10... | collective-permute-start | bytes 4718600 | tf_op jit(solution)/shard_map/ppermute | solution.py:20
  170.3 2.7 copy-start.2
  174.7 10.9 %slice-start = ((s8[6291456]{0:T(1024)(128)(4,1)}), s8[2097152]{0:T(1024)(128)(4,1)S(1)}, s32[]{:S(2)}) async-start(s8[6291456]{0:T(1024)(128)(4,1)} %bitcast.41), calls=%async_computation.5 | async-start | bytes 4194304
  176.1 9.6 %slice-start.1 = ((s8[6291456]{0:T(1024)(128)(4,1)}), s8[4194304]{0:T(1024)(128)(4,1)S(1)}, s32[]{:S(2)}) async-start(s8[6291456]{0:T(1024)(128)(4,1)} %bitcast.41), calls=%async_computation.6 | async-start | bytes 8388608
  261.3 15.8 %copy-start.4 = (bf16[1024,384]{1,0:T(8,128)(2,1)S(1)}, bf16[1024,384]{1,0:T(8,128)(2,1)}, u32[]{:S(2)}) copy-start(bf16[1024,384]{1,0:T(8,128)(2,1)} %shard_map.124) | copy-start | bytes 2359300
  283.8 1.1 copy-start.5
  283.9 193.2 %reduce-scatter.5.cloned.1.call-start = ((), (), s32[]{:S(2)}) async-start(), calls=%async_computation.4 | async-start | bytes 4718592 | tf_op jit(solution)/shard_map/reduce_scatter | solution.py:356
  285.0 23.9 %collective-permute-start.3 = (bf16[512,768]{1,0:T(8,128)(2,1)S(1)}, bf16[512,768]{1,0:T(8,128)(2,1)S(1)}, u32[]{:S(2)}, u32[]{:S(2)}) collective-permute-start(bf16[512,768]{1,0:T(8,128)(2,1)S(1)} %pad_maximum_fusion), channel_id=1, source_target_pairs={{30,0},{0,2},{2,4},{4,6},{6,8},{8,10},{10,12},{12,14},{14,16},{16,... | collective-permute-start | bytes 2359304 | tf_op jit(solution)/shard_map/ppermute | solution.py:20
  308.9 6.9 %copy-start.7 = (bf16[2,192,2304]{2,1,0:T(8,128)(2,1)S(1)}, bf16[2,192,2304]{2,1,0:T(8,128)(2,1)}, u32[]{:S(2)}) copy-start(bf16[2,192,2304]{2,1,0:T(8,128)(2,1)} %get-tuple-element.31) | copy-start | bytes 5308420
  315.7 45.3 %collective-permute-start.4 = (bf16[2,192,2304]{2,1,0:T(8,128)(2,1)}, bf16[2,192,2304]{2,1,0:T(8,128)(2,1)S(1)}, u32[]{:S(2)}, u32[]{:S(2)}) collective-permute-start(bf16[2,192,2304]{2,1,0:T(8,128)(2,1)} %get-tuple-element.29), channel_id=1, source_target_pairs={{30,0},{0,2},{2,4},{4,6},{6,8},{8,10},{10,12},{12,14},{14,16},{16,... | collective-permute-start | bytes 5308424 | tf_op jit(solution)/shard_map/ppermute | solution.py:20
  315.8 83.2 %collective-permute-start.5 = (bf16[2,192,2304]{2,1,0:T(8,128)(2,1)}, bf16[2,192,2304]{2,1,0:T(8,128)(2,1)S(1)}, u32[]{:S(2)}, u32[]{:S(2)}) collective-permute-start(bf16[2,192,2304]{2,1,0:T(8,128)(2,1)} %get-tuple-element.30), channel_id=1, source_target_pairs={{30,0},{0,2},{2,4},{4,6},{6,8},{8,10},{10,12},{12,14},{14,16},{16,... | collective-permute-start | bytes 5308424 | tf_op jit(solution)/shard_map/ppermute | solution.py:20
  315.9 121.0 %collective-permute-start.6 = (bf16[2,192,2304]{2,1,0:T(8,128)(2,1)S(1)}, bf16[2,192,2304]{2,1,0:T(8,128)(2,1)S(1)}, u32[]{:S(2)}, u32[]{:S(2)}) collective-permute-start(bf16[2,192,2304]{2,1,0:T(8,128)(2,1)S(1)} %copy-done.7), channel_id=1, source_target_pairs={{30,0},{0,2},{2,4},{4,6},{6,8},{8,10},{10,12},{12,14},{14,16},{16,... | collective-permute-start | bytes 5308424 | tf_op jit(solution)/shard_map/ppermute | solution.py:20
  315.9 157.7 %collective-permute-start.7 = (bf16[2,192,2304]{2,1,0:T(8,128)(2,1)}, bf16[2,192,2304]{2,1,0:T(8,128)(2,1)S(1)}, u32[]{:S(2)}, u32[]{:S(2)}) collective-permute-start(bf16[2,192,2304]{2,1,0:T(8,128)(2,1)} %get-tuple-element.32), channel_id=1, source_target_pairs={{30,0},{0,2},{2,4},{4,6},{6,8},{8,10},{10,12},{12,14},{14,16},{16,... | collective-permute-start | bytes 5308424 | tf_op jit(solution)/shard_map/ppermute | solution.py:20
  473.6 7.2 %copy-start.1 = (bf16[3072,4]{0,1:T(4,128)(2,1)S(1)}, bf16[3072,4]{0,1:T(4,128)(2,1)}, u32[]{:S(2)}) copy-start(bf16[3072,4]{0,1:T(4,128)(2,1)} %param.17) | copy-start | bytes 73732
Sparse Core Ops, SparseCore 0:
  112.8 113.2 all-gather.1
  284.0 15.0 reduce-scatter.2
  315.8 11.0 reduce-scatter.4
